TPU v7x, 256 devices: a whole 4x4x8 slice. The times are simulated.
256 devices in a mesh: pos: 32 (over x_lo, z, core), off: 8 (over x_hi, y).
Axes of the slice: x: 4 (x_hi: 2, x_lo: 2; x = x_hi * 2 + x_lo), y: 4, z: 8, core: 2. Of those that a mesh axis runs over, the one named last changes fastest.
Arguments:
- bin_embed: bfloat16 [2048, 128], P('pos'), may hold values from -6 to 6
- block_slot: int32 [32], replicated, may hold values from 0 to 31, each once
- proj_weight: bfloat16 [128, 64], replicated, may hold values from -0.5 to 0.5
- proj_bias: float32 [64], replicated, may hold values from -3 to 3
- conv_weight: bfloat16 [4, 576, 64], replicated, may hold values from -0.25 to 0.25
- conv_bias: float32 [4, 64], replicated, may hold values from -2 to 2
Outputs:
- contact: bfloat16 [32, 8, 64, 4096], P('pos', 'off')
Inputs may be any that keep to these rules, and one draw needn't show every extreme that they name: block_slot names every number of 0 to 31 once; bin block b's embeddings are rows block_slot[b] * 64 to block_slot[b] * 64 + 63 of bin_embed.
All inputs are finite; a program needn't handle non-finite values.
Results may differ from a plain program's by a relative error of at most 0.015.
Values may be sent and summed in bfloat16 or wider, within the bound.
A program may use at most 64 MiB of HBM per device.

v0:
```python
import functools

import jax
import jax.numpy as jnp
from jax import lax
from jax.experimental import pallas as pl
from jax.experimental.pallas import tpu as pltpu
from jax.sharding import PartitionSpec as P

TILE = 64
LAYERS = 4
HALO = 16
SIDE = TILE + 2 * HALO
END = HALO + TILE
PAD = 8
PITCH = SIDE + 2 * PAD
LANES = 128
MOST = 47
F32 = jnp.float32
BF16 = jnp.bfloat16

X_LO, Z, CORE = 2, 8, 2

OUTER = 0.7978845608028654
SCALE = (OUTER * 0.044715) ** (1 / 3)
INNER = OUTER / SCALE

ROWS = ((0, 96), (0, 96), (8, 88), (16, 80))
TURNS = ((5, 4, 3), (4, 4, 3), (4, 4, 2), (4, 3, 1))
SLOTS = (0, 2, 1, 3)
PARTS = 5


def low_half(shape):
    return lax.broadcasted_iota(jnp.int32, shape, 1) < LANES // 2


def swap(value):
    return pltpu.roll(value, LANES // 2, 1)


def halves(left, right):
    return jnp.where(low_half(left.shape), left, right)


def prepare_weights(conv, out):
    zero = jnp.zeros((TILE, TILE), BF16)
    blank = jnp.zeros((TILE, LANES), BF16)
    for layer in range(LAYERS):
        for row_tap in range(3):
            taps = [
                conv[layer, :, (3 * row_tap + j) * TILE : (3 * row_tap + j + 1) * TILE] * jnp.asarray(0.5, BF16)
                for j in range(3)
            ]
            pieces = {
                -1: jnp.concatenate([zero, taps[0]], axis=1),
                0: jnp.concatenate([taps[0], taps[1]], axis=1),
                1: jnp.concatenate([taps[1], taps[2]], axis=1),
                2: jnp.concatenate([taps[2], zero], axis=1),
            }
            for tile in range(3):
                part, side = divmod(3 * row_tap + tile, 2)
                for slot, column in enumerate(SLOTS):
                    piece = pieces.get(2 * tile - column, blank)
                    out[layer, part, slot * TILE : (slot + 1) * TILE, side * LANES : (side + 1) * LANES] = piece
        for slot in range(4):
            out[layer, PARTS - 1, slot * TILE : (slot + 1) * TILE, LANES:] = blank


def gather_kernel(
    embed_in,
    weight_in,
    conv_in,
    slots_in,
    bias_in,
    conv_bias_in,
    rows_out,
    cols_out,
    weights_out,
    bias_out,
    embed,
    weight,
    conv,
    slots,
    bias,
    conv_bias,
    bins,
    cols,
    local_sem,
    send_sem,
    recv_sem,
    twin_send,
    twin_recv,
):
    loads = [
        pltpu.make_async_copy(here, there, local_sem.at[k])
        for k, (here, there) in enumerate(
            (
                (embed_in, embed),
                (weight_in, weight),
                (conv_in, conv),
                (slots_in, slots),
                (bias_in, bias),
                (conv_bias_in, conv_bias),
            )
        )
    ]
    for load in loads:
        load.start()
    me = lax.axis_index("pos")
    offset = lax.axis_index("off")
    blocks = X_LO * Z * CORE
    x = me // (Z * CORE)
    z = (me // CORE) % Z
    core = me % CORE

    def index(across, along, core_):
        return (((x + across) % X_LO) * Z + (z + along) % Z) * CORE + core_

    order = [(across, along) for along in (4, 3, 5, 2, 6, 1, 7, 0) for across in (1, 0)][:-1]
    peers = [index(*step, core) for step in order]
    twin = index(0, 0, 1 - core)
    barrier = pltpu.get_barrier_semaphore()
    for peer in [*peers, twin]:
        pl.semaphore_signal(barrier, inc=1, device_id={"pos": peer}, device_id_type=pl.DeviceIdType.MESH)
    half = TILE // 2
    loads[0].wait()
    loads[1].wait()
    packed = [
        lax.dot_general(
            embed[part * half : (part + 1) * half],
            weight[...],
            (((1,), (1,)), ((), ())),
            preferred_element_type=F32,
        )
        for part in range(2)
    ]
    bins[me] = jnp.concatenate(packed, axis=1).astype(BF16)
    pl.semaphore_wait(barrier, len(peers) + 1)

    def send(block, peer, send_to, recv_from):
        copy = pltpu.make_async_remote_copy(
            src_ref=bins.at[block],
            dst_ref=bins.at[block],
            send_sem=send_to,
            recv_sem=recv_from,
            device_id={"pos": peer},
            device_id_type=pl.DeviceIdType.MESH,
        )
        copy.start()
        return copy

    direct = [send(me, peer, send_sem.at[k], recv_sem.at[k]) for k, peer in enumerate(peers)]
    passed = [send(me, twin, twin_send.at[len(order)], twin_recv.at[len(order)])]
    for load in loads[2:]:
        load.wait()
    prepare_weights(conv, weights_out)
    bias_out[0:LAYERS] = SCALE * jnp.concatenate([conv_bias[...], conv_bias[...]], axis=1)
    for k, (across, along) in enumerate(order):
        direct[k].wait_recv()
        block = index(across, Z - along, core)
        passed.append(send(block, twin, twin_send.at[k], twin_recv.at[k]))
    for copy in passed:
        copy.wait_recv()
    for copy in [*direct, *passed]:
        copy.wait_send()

    def spread(base, out):
        def block(shift):
            return bins[slots[(base + shift + blocks) % blocks]].astype(F32) * SCALE

        before, here, after = block(-1), block(0), block(1)
        tail, head = before[half - HALO :], after[:HALO]
        out[0:HALO] = halves(swap(tail), tail)
        out[HALO : HALO + half] = halves(here, swap(here))
        out[HALO + half : END] = halves(swap(here), here)
        out[END:SIDE] = halves(head, swap(head))

    spread(me, rows_out)
    spread(me + offset, cols)
    left = cols[pl.ds(1, MOST, stride=2), :]
    right = cols[pl.ds(2, MOST, stride=2), :]
    cols_out[0:MOST] = halves(left, right) + SCALE * jnp.concatenate([bias[...], bias[...]], axis=1)


def hide(value):
    return value + value * jnp.tanh(value * (INNER + value * value))


def at(tile, row):
    return tile * PITCH + PAD + row


def keep_band(value, first, left, right, inside, corner):
    def factor(limits):
        kinds = [limits(left), limits(right)]
        if kinds == [None, None] or inside is None:
            return None
        rows = [jnp.ones((1, LANES), F32) if kind is None else kind for kind in kinds]
        return rows[0] if kinds[0] is kinds[1] else halves(*rows)

    top = factor(lambda column: None if column < HALO else inside if column < END else corner)
    middle = factor(lambda column: None if column < END else inside)
    pieces = []
    for low, high, scale in ((0, HALO, top), (HALO, END, middle), (END, SIDE, None)):
        low, high = max(low, first) - first, min(high - first, value.shape[0])
        if low < high:
            piece = value[low:high]
            pieces.append(piece if scale is None else piece * scale)
    return jnp.concatenate(pieces, axis=0)


def turned(hidden, tiles, row):
    block = jnp.stack([hidden[pl.ds(at(tile, row), 8), :] for tile in tiles], axis=0)
    block = jnp.swapaxes(block, 0, 1)
    return [block[k] for k in range(8)]


def target_columns(d, shift):
    groups = (SIDE - 2 * d) // (2 * d)
    span = max(8, 2 * d)
    for start in range(d, SIDE - d, span):
        places = []
        for column in range(start, min(start + span, SIDE - d)):
            group, inner = divmod(column - d, 2 * d)
            if inner < d:
                places.append((group * d + inner, column, column - start, column - start + d))
        yield [start + shift + 8 * k for k in range(span // 8)], places


def source_bundles(d, shift):
    groups = (SIDE - 2 * d) // (2 * d)
    if d == 2:
        for inner in range(d):
            for first in range(0, groups, 8):
                count = min(8, groups - first)
                tiles = [min(first + k, groups - 1) * d + inner for k in range(8)]
                rows = d + 2 * d * first + inner + shift
                yield tiles, [(half, 0, count, rows + half * d, 2 * d) for half in range(2)]
        return
    step = 8 // d
    for first in range(0, groups, step):
        tiles = [min(first + k // d, groups - 1) * d + k % d for k in range(8)]
        runs = []
        for k in range(min(step, groups - first)):
            rows = d + 2 * d * (first + k) + shift
            runs += [(half, k * d, d, rows + half * d, 1) for half in range(2)]
        yield tiles, runs


def clip(run, low, high):
    half, place, count, row, stride = run
    skip = max(0, -((row - low) // stride))
    stop = min(count, -((row - high) // stride))
    return half, place + skip, stop - skip, row + skip * stride, stride


def mirror(hidden, d, columns, rows, shift, keep=None):
    for tiles, runs in source_bundles(d, shift):
        runs = [clip(run, *rows) for run in runs]
        runs = [run for run in runs if run[2] > 0]
        if not runs:
            continue
        for reads, places in target_columns(d, shift):
            places = [p for p in places if p[1] + d >= columns[0] and p[1] < columns[1]]
            if not places:
                continue
            lines = {}
            for k, row in enumerate(reads):
                if any(p[2] // 8 == k or (p[3] // 8 == k and p[1] + d < columns[1]) for p in places):
                    for n, line in enumerate(turned(hidden, tiles, row)):
                        lines[8 * k + n] = line
            for tile, column, one, two in places:
                straddles = column + d >= columns[1]
                values = {}
                for half, place, count, row, stride in runs:
                    if half not in values:
                        if straddles:
                            values[half] = lines[one] if half == 0 else swap(lines[one])
                        elif half == 0:
                            values[half] = halves(lines[one], swap(lines[two]))
                        else:
                            values[half] = halves(swap(lines[one]), lines[two])
                    value = values[half][place : place + count]
                    goal = pl.ds(at(tile, row), count, stride=stride) if stride > 1 else pl.ds(at(tile, row), count)
                    if straddles or keep is not None:
                        old = hidden[goal, :]
                        if straddles:
                            value = halves(value, old)
                        if keep is not None:
                            value = jnp.where(jnp.broadcast_to(keep, value.shape) > 0, old, value)
                    hidden[goal, :] = value


def weave(main, side):
    done = 0
    for k, unit in enumerate(main):
        unit()
        upto = len(side) * (k + 1) // len(main)
        for extra in side[done:upto]:
            extra()
        done = upto
    for extra in side[done:]:
        extra()


def conv_kernel(bands, rows, cols, weights, bias, out, *scratch):
    offset = lax.axis_index("off")

    @pl.when(offset == 0)
    def _():
        conv_layers(bands, offset, True, rows, cols, weights, bias, out, *scratch)

    @pl.when(offset > 0)
    def _():
        conv_layers(bands, offset, False, rows, cols, weights, bias, out, *scratch)


def conv_layers(bands, offset, diagonal, rows, cols, weights, bias, out, state_a, state_b, hidden_a, hidden_b):
    def flag(holds):
        return jnp.broadcast_to(holds.astype(F32), (1, LANES))

    if diagonal:
        inside = corner = None
    else:
        inside, corner = flag(offset < bands - 1), flag(offset < bands - 2)
    keep = flag(offset != 1)

    def start(tile):
        value = rows[...] + cols[tile : tile + 1, :]
        state_a[tile] = value
        hidden_a[pl.ds(at(tile, 0), SIDE), :] = keep_band(hide(value), 0, 2 * tile + 1, 2 * tile + 2, inside, corner)

    source, target = (state_a, hidden_a), (state_b, hidden_b)
    for layer in range(LAYERS):
        conv_layer(layer, diagonal, source, target, weights.at[layer], bias[layer : layer + 1], out, inside, corner, start)
        d = 2 ** (layer + 1)
        if layer == LAYERS - 1:
            break
        if diagonal:
            mirror(target[1], d, (d, HALO), (HALO, SIDE - d), 0)
            mirror(target[1], d, (HALO, END), (END, SIDE - d), 0)
        else:
            mirror(target[1], d, (d, HALO), (END, SIDE - d), TILE, keep)
        source, target = target, source


def rows_of(layer, diagonal, quad):
    first, last = ROWS[layer]
    k, i = quad
    d = 2**layer
    column = 2 * d + 4 * d * k + i
    if diagonal and column + 3 * d < HALO:
        last = min(last, HALO)
    elif diagonal and column + 3 * d < END:
        last = min(last, END)
    if (last - first) % 16:
        return ROWS[layer]
    return first, last


def conv_layer(layer, diagonal, source, target, weights, bias, out, inside, corner, start):
    state, hidden = source
    next_state, next_hidden = target
    d = 2**layer
    quads = [(k, i) for k in range((SIDE - 4 * d) // (4 * d)) for i in range(d)]
    spans = {quad: rows_of(layer, diagonal, quad) for quad in quads}
    turns, begin = [], 0
    for size in TURNS[layer]:
        turns.append(quads[begin : begin + 2 * size])
        begin += 2 * size
    kinds, places = [], {}
    for turn, members in enumerate(turns):
        used = []
        for place, quad in enumerate(members):
            kind = (place % 2, turn % 2, spans[quad][1] - spans[quad][0])
            count = used.count(kind)
            used.append(kind)
            places[turn, place] = (*kind, count)
    kinds = sorted(set(places.values()))

    def inputs(quad):
        k, i = quad
        return [(2 * k + step) * d + i for step in range(3)]

    def body(*accs):
        accs = dict(zip(kinds, accs))

        def push(part):
            for mxu in range(2):
                pltpu.matmul_push_rhs(weights[part], part % 2, mxu, transpose=True)

        def multiply(turn, part, place):
            quad = turns[turn][place]
            tiles = inputs(quad)
            first, last = spans[quad]
            pieces = []
            for step in (2 * part, min(2 * part + 1, 8)):
                row_tap, tile = divmod(step, 3)
                pieces.append(hidden[pl.ds(at(tiles[tile], first + (row_tap - 1) * d), last - first), :])
            lhs = jnp.concatenate(pieces, axis=1).astype(BF16)
            pltpu.matmul_acc_lhs(accs[places[turn, place]], lhs, part % 2 if place < 2 else None)

        def issue(turn):
            units = []
            for part in range(PARTS):
                units.append(functools.partial(push, part))
                units += [functools.partial(multiply, turn, part, place) for place in range(len(turns[turn]))]
            return units

        def sums(turn, place):
            quad = turns[turn][place]
            first, last = spans[quad]
            summed = pltpu.matmul_pop(accs[places[turn, place]])
            before, here, after = [state[tile, first:last] for tile in inputs(quad)]
            return [
                summed[:, :LANES] + (halves(swap(before), here) + bias),
                summed[:, LANES:] + (halves(here, swap(after)) + bias),
            ]

        def finish(turn, place):
            quad = turns[turn][place]
            k, i = quad
            first, last = spans[quad]
            for step, value in enumerate(sums(turn, place)):
                column = 2 * d + 4 * d * k + i + step * d
                tile = k * 2 * d + i + step * d
                next_state[tile, first:last] = value
                next_hidden[pl.ds(at(tile, first), last - first), :] = keep_band(
                    hide(value), first, column, column + 2 * d, inside, corner
                )

        def finish_out(turn, place):
            k, i = turns[turn][place]
            for step, (even, odd) in enumerate(zip(sums(turn, place), sums(turn, place + 1))):
                even, odd = even * (1 / SCALE), odd * (1 / SCALE)
                for far, value in enumerate((halves(even, swap(odd)), halves(swap(even), odd))):
                    column = 4 * d * k + i + step * d + far * 2 * d
                    out[0, 0, :, column * TILE : column * TILE + LANES] = value.astype(BF16)

        def ends(turn):
            if layer == LAYERS - 1:
                return [functools.partial(finish_out, turn, place) for place in range(0, len(turns[turn]), 2)]
            return [functools.partial(finish, turn, place) for place in range(len(turns[turn]))]

        ready = 0
        for turn in range(len(turns)):
            side = []
            if layer == 0:
                if turn == 0:
                    ready = inputs(turns[0][-1])[-1] + 1
                    for tile in range(ready):
                        start(tile)
                upto = inputs(turns[turn + 1][-1])[-1] + 1 if turn + 1 < len(turns) else ready
                side += [functools.partial(start, tile) for tile in range(ready, upto)]
                ready = upto
            if turn > 0:
                side += ends(turn - 1)
            weave(issue(turn), side)
        for unit in ends(len(turns) - 1):
            unit()

    pl.run_scoped(body, *[pltpu.ACC(mxu)((height, 256), F32) for mxu, _, height, _ in kinds])


def vmem(count):
    return [pl.BlockSpec(memory_space=pltpu.VMEM)] * count


def on_device(bands, bin_embed, block_slot, proj_weight, proj_bias, conv_weight, conv_bias):
    blocks = block_slot.shape[0]
    inputs = [bin_embed, proj_weight.T, jnp.swapaxes(conv_weight, 1, 2), block_slot, proj_bias.reshape(1, -1), conv_bias]
    ready = pl.pallas_call(
        gather_kernel,
        name="gather_bins",
        out_shape=[
            pltpu.VMEM((SIDE, LANES), F32),
            pltpu.VMEM((MOST + 1, LANES), F32),
            pltpu.VMEM((LAYERS, PARTS, 256, 256), BF16),
            pltpu.VMEM((8, LANES), F32),
        ],
        in_specs=[pl.BlockSpec(memory_space=pltpu.HBM)] * len(inputs),
        out_specs=vmem(4),
        scratch_shapes=[
            *[
                (pltpu.SMEM if value is block_slot else pltpu.VMEM)(value.shape, value.dtype)
                for value in inputs
            ],
            pltpu.VMEM((blocks, TILE // 2, LANES), BF16),
            pltpu.VMEM((SIDE, LANES), F32),
            pltpu.SemaphoreType.DMA((len(inputs),)),
            *[pltpu.SemaphoreType.DMA((blocks // CORE,))] * 4,
        ],
        compiler_params=pltpu.CompilerParams(collective_id=0, has_side_effects=True, vmem_limit_bytes=32 * 2**20),
    )(*[pltpu.with_memory_space_constraint(value, pltpu.HBM) for value in inputs])
    ready = [pltpu.with_memory_space_constraint(value, pltpu.VMEM) for value in ready]
    return pl.pallas_call(
        functools.partial(conv_kernel, bands),
        name="conv_tiles",
        out_shape=jax.ShapeDtypeStruct((1, 1, TILE, TILE * TILE), BF16),
        in_specs=vmem(4),
        out_specs=vmem(1)[0],
        scratch_shapes=[
            *[pltpu.VMEM((MOST, SIDE, LANES), F32)] * 2,
            *[pltpu.VMEM((MOST * PITCH, LANES), F32)] * 2,
        ],
        compiler_params=pltpu.CompilerParams(vmem_limit_bytes=32 * 2**20),
    )(*ready)


def solution(mesh):
    placed = (P("pos", None), P(), P(), P(), P(), P())
    return jax.shard_map(
        functools.partial(on_device, mesh.shape["off"]),
        mesh=mesh,
        in_specs=placed,
        out_specs=P("pos", "off", None, None),
        check_vma=False,
    )
```

profile of v0, /device:TPU:1, one launch (start us, length us, event | category | flops | bytes accessed | tf_op | source)
XLA Modules:
  0.0 23.5 jit_solution(5640094179451867931)
XLA Ops:
  0.0 15.9 %gather_bins.1 = (f32[96,128]{1,0:T(8,128)S(1)}, f32[48,128]{1,0:T(8,128)S(1)}, bf16[4,5,256,256]{3,2,1,0:T(8,128)(2,1)S(1)}, f32[8,128]{1,0:T(8,128)S(1)}) custom-call(bf16[64,128]{1,0:T(8,128)(2,1)} %embed_in.1, bf16[64,128]{1,0:T(8,128)(2,1)} %bitcast.4, bf16[4,64,576]{2,1,0:T(8,128)(2,1)} %bitcast.3, s32[32]{0:T(128)} %slots_in.1, f32[1,64]{1,0:T(1,128)} %bitcast.5, ...), custom_call_target="tpu_custom_call" | custom-call | tf_op jit(solution)/shard_map/gather_bins/pallas_call | solution.py:473
  15.9 7.6 %conv_tiles.1 = bf16[1,1,64,4096]{3,2,1,0:T(8,128)(2,1)} custom-call(f32[96,128]{1,0:T(8,128)S(1)} %get-tuple-element.9.rows, f32[48,128]{1,0:T(8,128)S(1)} %get-tuple-element.10.cols, bf16[4,5,256,256]{3,2,1,0:T(8,128)(2,1)S(1)} %get-tuple-element.11.weights, f32[8,128]{1,0:T(8,128)S(1)} %get-tuple-element.12.bias), custom_call_target="tpu_custom_call" | custom-call | tf_op jit(solution)/shard_map/conv_tiles/pallas_call | solution.py:497
where the time goes:
time: 23.7 us; the launch traced here: 23.5 us
  Pallas kernels  23.5 us (99%)
    pallas_call x1, Pallas kernels, on_device(): pl.pallas_call(gather_kernel, name='gather_bins', out_shape=[pltpu.VMEM((...  15.9 us
    pallas_call x1, Pallas kernels, on_device(): pl.pallas_call(functools.partial(conv_kernel, bands), name='conv_tiles',...  7.63 us

commit v1 on v0

--- a/solution.py
+++ b/solution.py
@@ -20,13 +20,14 @@
 BF16 = jnp.bfloat16
 
 X_LO, Z, CORE = 2, 8, 2
+NEAR = 4
 
 OUTER = 0.7978845608028654
 SCALE = (OUTER * 0.044715) ** (1 / 3)
 INNER = OUTER / SCALE
 
 ROWS = ((0, 96), (0, 96), (8, 88), (16, 80))
-TURNS = ((5, 4, 3), (4, 4, 3), (4, 4, 2), (4, 3, 1))
+TURNS = ((4, 4, 4), (4, 4, 3), (5, 5), (4, 4))
 SLOTS = (0, 2, 1, 3)
 PARTS = 5
 
@@ -91,6 +92,8 @@
     recv_sem,
     twin_send,
     twin_recv,
+    ready_sem,
+    all_sem,
 ):
     loads = [
         pltpu.make_async_copy(here, there, local_sem.at[k])
@@ -113,62 +116,134 @@
     x = me // (Z * CORE)
     z = (me // CORE) % Z
     core = me % CORE
-
-    def index(across, along, core_):
-        return (((x + across) % X_LO) * Z + (z + along) % Z) * CORE + core_
-
-    order = [(across, along) for along in (4, 3, 5, 2, 6, 1, 7, 0) for across in (1, 0)][:-1]
-    peers = [index(*step, core) for step in order]
-    twin = index(0, 0, 1 - core)
+    twin = me + 1 - 2 * core
+    near = z < NEAR
+
+    def index(across, along):
+        return (across * Z + along) * CORE + core
+
+    def other(across):
+        return (x + across) % X_LO
+
+    def place(block):
+        return block // CORE
+
+    near_chips = [(across, along) for along in range(NEAR) for across in range(X_LO)]
+    far_chips = [(across, along) for along in range(NEAR, Z) for across in range(X_LO)]
+    partner = Z - 1 - z
     barrier = pltpu.get_barrier_semaphore()
-    for peer in [*peers, twin]:
-        pl.semaphore_signal(barrier, inc=1, device_id={"pos": peer}, device_id_type=pl.DeviceIdType.MESH)
-    half = TILE // 2
-    loads[0].wait()
-    loads[1].wait()
-    packed = [
-        lax.dot_general(
-            embed[part * half : (part + 1) * half],
-            weight[...],
-            (((1,), (1,)), ((), ())),
-            preferred_element_type=F32,
-        )
-        for part in range(2)
-    ]
-    bins[me] = jnp.concatenate(packed, axis=1).astype(BF16)
-    pl.semaphore_wait(barrier, len(peers) + 1)
-
-    def send(block, peer, send_to, recv_from):
-        copy = pltpu.make_async_remote_copy(
+
+    def greet(peer, semaphore):
+        pl.semaphore_signal(semaphore, inc=1, device_id={"pos": peer}, device_id_type=pl.DeviceIdType.MESH)
+
+    def copy(block, peer, sends, receives):
+        return pltpu.make_async_remote_copy(
             src_ref=bins.at[block],
             dst_ref=bins.at[block],
-            send_sem=send_to,
-            recv_sem=recv_from,
+            send_sem=sends,
+            recv_sem=receives,
             device_id={"pos": peer},
             device_id_type=pl.DeviceIdType.MESH,
         )
-        copy.start()
-        return copy
-
-    direct = [send(me, peer, send_sem.at[k], recv_sem.at[k]) for k, peer in enumerate(peers)]
-    passed = [send(me, twin, twin_send.at[len(order)], twin_recv.at[len(order)])]
-    for load in loads[2:]:
-        load.wait()
-    prepare_weights(conv, weights_out)
-    bias_out[0:LAYERS] = SCALE * jnp.concatenate([conv_bias[...], conv_bias[...]], axis=1)
-    for k, (across, along) in enumerate(order):
-        direct[k].wait_recv()
-        block = index(across, Z - along, core)
-        passed.append(send(block, twin, twin_send.at[k], twin_recv.at[k]))
-    for copy in passed:
-        copy.wait_recv()
-    for copy in [*direct, *passed]:
-        copy.wait_send()
+
+    def to_peer(block, peer):
+        return copy(block, peer, send_sem.at[place(peer)], recv_sem.at[place(block)])
+
+    def to_twin(block):
+        return copy(block, twin, twin_send.at[place(block)], twin_recv.at[place(block)])
+
+    def project():
+        half = TILE // 2
+        loads[0].wait()
+        loads[1].wait()
+        packed = [
+            lax.dot_general(
+                embed[part * half : (part + 1) * half],
+                weight[...],
+                (((1,), (1,)), ((), ())),
+                preferred_element_type=F32,
+            )
+            for part in range(2)
+        ]
+        bins[me] = jnp.concatenate(packed, axis=1).astype(BF16)
+
+    def prepare():
+        for load in loads[2:]:
+            load.wait()
+        prepare_weights(conv, weights_out)
+        bias_out[0:LAYERS] = SCALE * jnp.concatenate([conv_bias[...], conv_bias[...]], axis=1)
+
+    def chips_by_distance():
+        flip = jnp.logical_or(z < NEAR // 2, z >= Z - NEAR // 2)
+        return [(across, jnp.where(flip, Z - 1 - k, NEAR + k)) for k in range(Z - NEAR) for across in (x, 1 - x)]
+
+    def each(chips, act):
+        for across, along in chips:
+            act(index(across, along))
+
+    def others(chips, act):
+        for across, along in chips:
+            block = index(across, along)
+
+            @pl.when(block != me)
+            def _():
+                act(block)
+
+    def arrive(block):
+        to_peer(block, me).wait_recv()
+
+    greet(twin, barrier)
+
+    @pl.when(near)
+    def _():
+        others(near_chips, lambda peer: greet(peer, barrier))
+        each(far_chips, lambda peer: greet(peer, barrier))
+        project()
+        pl.semaphore_wait(barrier, len(near_chips))
+        others(near_chips, lambda peer: to_peer(me, peer).start())
+        to_twin(me).start()
+
+    @pl.when(jnp.logical_not(near))
+    def _():
+        project()
+        pl.semaphore_wait(barrier, len(near_chips) + 1)
+        each(near_chips, lambda peer: to_peer(me, peer).start())
+        each(near_chips, lambda peer: greet(peer, ready_sem))
+        to_twin(me).start()
+
+    prepare()
+
+    def pass_on(block):
+        arrive(block)
+        to_twin(block).start()
+
+    @pl.when(near)
+    def _():
+        others(near_chips, pass_on)
+        pl.semaphore_wait(ready_sem, len(far_chips))
+        greet(index(x, partner), all_sem)
+        each(far_chips, lambda peer: to_peer(me, peer).start())
+        each(chips_by_distance(), pass_on)
+
+    @pl.when(jnp.logical_not(near))
+    def _():
+        pl.semaphore_wait(all_sem, 1)
+        others(far_chips, lambda peer: to_peer(me, peer).start())
+        each(near_chips, pass_on)
+        others(far_chips, pass_on)
+
+    for chip in range(blocks // CORE):
+        to_twin(2 * chip + 1 - core).wait_recv()
+    for chip in range(blocks // CORE):
+        to_twin(2 * chip + core).wait_send()
+    others(near_chips, lambda peer: to_peer(me, peer).wait_send())
+    others(far_chips, lambda peer: to_peer(me, peer).wait_send())
 
     def spread(base, out):
         def block(shift):
             return bins[slots[(base + shift + blocks) % blocks]].astype(F32) * SCALE
 
+        half = TILE // 2
         before, here, after = block(-1), block(0), block(1)
         tail, head = before[half - HALO :], after[:HALO]
         out[0:HALO] = halves(swap(tail), tail)
@@ -304,16 +379,41 @@
         extra()
 
 
-def conv_kernel(bands, rows, cols, weights, bias, out, *scratch):
+class Writer:
+    def __init__(self, out, staged, sems):
+        self.out, self.staged, self.sems = out, staged, sems
+        self.waiting, self.started = [], []
+
+    def put(self, pair, value):
+        self.staged[:, pair * LANES : (pair + 1) * LANES] = value
+        self.waiting.append(pair)
+
+    def copy(self, pair):
+        lanes = slice(pair * LANES, (pair + 1) * LANES)
+        return pltpu.make_async_copy(self.staged.at[:, lanes], self.out.at[0, 0, :, lanes], self.sems.at[pair])
+
+    def flush(self):
+        for pair in self.waiting:
+            self.copy(pair).start()
+        self.started += self.waiting
+        self.waiting = []
+
+    def end(self):
+        self.flush()
+        for pair in self.started:
+            self.copy(pair).wait()
+
+
+def conv_kernel(bands, rows, cols, weights, bias, out, staged, sems, *scratch):
     offset = lax.axis_index("off")
 
     @pl.when(offset == 0)
     def _():
-        conv_layers(bands, offset, True, rows, cols, weights, bias, out, *scratch)
+        conv_layers(bands, offset, True, rows, cols, weights, bias, Writer(out, staged, sems), *scratch)
 
     @pl.when(offset > 0)
     def _():
-        conv_layers(bands, offset, False, rows, cols, weights, bias, out, *scratch)
+        conv_layers(bands, offset, False, rows, cols, weights, bias, Writer(out, staged, sems), *scratch)
 
 
 def conv_layers(bands, offset, diagonal, rows, cols, weights, bias, out, state_a, state_b, hidden_a, hidden_b):
@@ -336,6 +436,7 @@
         conv_layer(layer, diagonal, source, target, weights.at[layer], bias[layer : layer + 1], out, inside, corner, start)
         d = 2 ** (layer + 1)
         if layer == LAYERS - 1:
+            out.end()
             break
         if diagonal:
             mirror(target[1], d, (d, HALO), (HALO, SIDE - d), 0)
@@ -432,11 +533,12 @@
 
         def finish_out(turn, place):
             k, i = turns[turn][place]
+            out.flush()
             for step, (even, odd) in enumerate(zip(sums(turn, place), sums(turn, place + 1))):
                 even, odd = even * (1 / SCALE), odd * (1 / SCALE)
                 for far, value in enumerate((halves(even, swap(odd)), halves(swap(even), odd))):
                     column = 4 * d * k + i + step * d + far * 2 * d
-                    out[0, 0, :, column * TILE : column * TILE + LANES] = value.astype(BF16)
+                    out.put(column // 2, value.astype(BF16))
 
         def ends(turn):
             if layer == LAYERS - 1:
@@ -490,6 +592,7 @@
             pltpu.VMEM((SIDE, LANES), F32),
             pltpu.SemaphoreType.DMA((len(inputs),)),
             *[pltpu.SemaphoreType.DMA((blocks // CORE,))] * 4,
+            *[pltpu.SemaphoreType.REGULAR] * 2,
         ],
         compiler_params=pltpu.CompilerParams(collective_id=0, has_side_effects=True, vmem_limit_bytes=32 * 2**20),
     )(*[pltpu.with_memory_space_constraint(value, pltpu.HBM) for value in inputs])
@@ -499,8 +602,10 @@
         name="conv_tiles",
         out_shape=jax.ShapeDtypeStruct((1, 1, TILE, TILE * TILE), BF16),
         in_specs=vmem(4),
-        out_specs=vmem(1)[0],
+        out_specs=pl.BlockSpec(memory_space=pl.ANY),
         scratch_shapes=[
+            pltpu.VMEM((TILE, TILE * TILE), BF16),
+            pltpu.SemaphoreType.DMA((TILE // 2,)),
             *[pltpu.VMEM((MOST, SIDE, LANES), F32)] * 2,
             *[pltpu.VMEM((MOST * PITCH, LANES), F32)] * 2,
         ],

time: 23.7 us -> 22.8 us (0.962)
  the two profiles are of different devices: /device:TPU:1 before, /device:TPU:233 now
where the time goes in v1:
time: 22.8 us; the launch traced here: 22.6 us
  Pallas kernels  22.5 us (99%)
    pallas_call x1, Pallas kernels, on_device(): pl.pallas_call(gather_kernel, name='gather_bins', out_shape=[pltpu.VMEM((...  14.7 us
    pallas_call x1, Pallas kernels, on_device(): pl.pallas_call(functools.partial(conv_kernel, bands), name='conv_tiles',...  7.72 us

profile of v1, /device:TPU:233, one launch (start us, length us, event | category | flops | bytes accessed | tf_op | source)
XLA Modules:
  0.0 22.6 jit_solution(9268390199510410607)
XLA Ops:
  0.0 14.7 %gather_bins.1 = (f32[96,128]{1,0:T(8,128)S(1)}, f32[48,128]{1,0:T(8,128)S(1)}, bf16[4,5,256,256]{3,2,1,0:T(8,128)(2,1)S(1)}, f32[8,128]{1,0:T(8,128)S(1)}) custom-call(bf16[64,128]{1,0:T(8,128)(2,1)} %embed_in.1, bf16[64,128]{1,0:T(8,128)(2,1)} %bitcast.4, bf16[4,64,576]{2,1,0:T(8,128)(2,1)} %bitcast.3, s32[32]{0:T(128)} %slots_in.1, f32[1,64]{1,0:T(1,128)} %bitcast.5, ...), custom_call_target="tpu_custom_call" | custom-call | tf_op jit(solution)/shard_map/gather_bins/pallas_call | solution.py:575
  14.7 7.7 %conv_tiles.1 = bf16[1,1,64,4096]{3,2,1,0:T(8,128)(2,1)} custom-call(f32[96,128]{1,0:T(8,128)S(1)} %get-tuple-element.9.rows, f32[48,128]{1,0:T(8,128)S(1)} %get-tuple-element.10.cols, bf16[4,5,256,256]{3,2,1,0:T(8,128)(2,1)S(1)} %get-tuple-element.11.weights, f32[8,128]{1,0:T(8,128)S(1)} %get-tuple-element.12.bias), custom_call_target="tpu_custom_call" | custom-call | tf_op jit(solution)/shard_map/conv_tiles/pallas_call | solution.py:600

commit v2 on v1

--- a/solution.py
+++ b/solution.py
@@ -129,8 +129,7 @@
         return block // CORE
 
     near_chips = [(across, along) for along in range(NEAR) for across in range(X_LO)]
-    far_chips = [(across, along) for along in range(NEAR, Z) for across in range(X_LO)]
-    partner = Z - 1 - z
+    far_chips = [(across, along) for along in (7, 6, 4, 5) for across in range(X_LO)]
     barrier = pltpu.get_barrier_semaphore()
 
     def greet(peer, semaphore):
@@ -221,7 +220,15 @@
     def _():
         others(near_chips, pass_on)
         pl.semaphore_wait(ready_sem, len(far_chips))
-        greet(index(x, partner), all_sem)
+
+        @pl.when(z == 0)
+        def _():
+            each([(x, along) for along in range(NEAR + 2, Z)], lambda peer: greet(peer, all_sem))
+
+        @pl.when(z == NEAR - 1)
+        def _():
+            each([(x, along) for along in range(NEAR, NEAR + 2)], lambda peer: greet(peer, all_sem))
+
         each(far_chips, lambda peer: to_peer(me, peer).start())
         each(chips_by_distance(), pass_on)
 
@@ -229,8 +236,8 @@
     def _():
         pl.semaphore_wait(all_sem, 1)
         others(far_chips, lambda peer: to_peer(me, peer).start())
+        others(far_chips, pass_on)
         each(near_chips, pass_on)
-        others(far_chips, pass_on)
 
     for chip in range(blocks // CORE):
         to_twin(2 * chip + 1 - core).wait_recv()
@@ -407,13 +414,13 @@
 def conv_kernel(bands, rows, cols, weights, bias, out, staged, sems, *scratch):
     offset = lax.axis_index("off")
 
+    @pl.when(offset > 0)
+    def _():
+        conv_layers(bands, offset, False, rows, cols, weights, bias, Writer(out, staged, sems), *scratch)
+
     @pl.when(offset == 0)
     def _():
         conv_layers(bands, offset, True, rows, cols, weights, bias, Writer(out, staged, sems), *scratch)
-
-    @pl.when(offset > 0)
-    def _():
-        conv_layers(bands, offset, False, rows, cols, weights, bias, Writer(out, staged, sems), *scratch)
 
 
 def conv_layers(bands, offset, diagonal, rows, cols, weights, bias, out, state_a, state_b, hidden_a, hidden_b):

time: 22.8 us -> 22 us (0.965)
  Pallas kernels: 22.5 us -> 21.7 us
    pallas_call x1, Pallas kernels: 14.7 us -> 14 us  [on_device(): pl.pallas_call(gather_kernel, name='gather_bins', out_shape=[pltpu.VMEM((...]
where the time goes in v2:
time: 22 us; the launch traced here: 21.8 us
  Pallas kernels  21.7 us (99%)
    pallas_call x1, Pallas kernels, on_device(): pl.pallas_call(gather_kernel, name='gather_bins', out_shape=[pltpu.VMEM((...  14 us
    pallas_call x1, Pallas kernels, on_device(): pl.pallas_call(functools.partial(conv_kernel, bands), name='conv_tiles',...  7.69 us

profile of v2, /device:TPU:233, one launch (start us, length us, event | category | flops | bytes accessed | tf_op | source)
XLA Modules:
  0.0 21.8 jit_solution(6017112165107819613)
XLA Ops:
  0.0 14.0 %gather_bins.1 = (f32[96,128]{1,0:T(8,128)S(1)}, f32[48,128]{1,0:T(8,128)S(1)}, bf16[4,5,256,256]{3,2,1,0:T(8,128)(2,1)S(1)}, f32[8,128]{1,0:T(8,128)S(1)}) custom-call(bf16[64,128]{1,0:T(8,128)(2,1)} %embed_in.1, bf16[64,128]{1,0:T(8,128)(2,1)} %bitcast.4, bf16[4,64,576]{2,1,0:T(8,128)(2,1)} %bitcast.3, s32[32]{0:T(128)} %slots_in.1, f32[1,64]{1,0:T(1,128)} %bitcast.5, ...), custom_call_target="tpu_custom_call" | custom-call | tf_op jit(solution)/shard_map/gather_bins/pallas_call | solution.py:582
  14.0 7.7 %conv_tiles.1 = bf16[1,1,64,4096]{3,2,1,0:T(8,128)(2,1)} custom-call(f32[96,128]{1,0:T(8,128)S(1)} %get-tuple-element.9.rows, f32[48,128]{1,0:T(8,128)S(1)} %get-tuple-element.10.cols, bf16[4,5,256,256]{3,2,1,0:T(8,128)(2,1)S(1)} %get-tuple-element.11.weights, f32[8,128]{1,0:T(8,128)S(1)} %get-tuple-element.12.bias), custom_call_target="tpu_custom_call" | custom-call | tf_op jit(solution)/shard_map/conv_tiles/pallas_call | solution.py:607

commit v3 on v2

--- a/solution.py
+++ b/solution.py
@@ -44,7 +44,9 @@
     return jnp.where(low_half(left.shape), left, right)
 
 
-def prepare_weights(conv, out):
+def prepare_weights(conv, bias, out):
+    eye = lax.broadcasted_iota(jnp.int32, (TILE, TILE), 0) == lax.broadcasted_iota(jnp.int32, (TILE, TILE), 1)
+    lane = lax.broadcasted_iota(jnp.int32, (TILE, LANES), 1)
     zero = jnp.zeros((TILE, TILE), BF16)
     blank = jnp.zeros((TILE, LANES), BF16)
     for layer in range(LAYERS):
@@ -64,8 +66,12 @@
                 for slot, column in enumerate(SLOTS):
                     piece = pieces.get(2 * tile - column, blank)
                     out[layer, part, slot * TILE : (slot + 1) * TILE, side * LANES : (side + 1) * LANES] = piece
+        whole = SCALE * bias[layer : layer + 1, :]
+        high = whole.astype(BF16).astype(F32)
+        terms = [jnp.sum(jnp.where(eye, term, 0.0), axis=1, keepdims=True) for term in (high, whole - high)]
+        shift = jnp.where(lane == 0, terms[0], jnp.where(lane == 1, terms[1], 0.0)).astype(BF16)
         for slot in range(4):
-            out[layer, PARTS - 1, slot * TILE : (slot + 1) * TILE, LANES:] = blank
+            out[layer, PARTS - 1, slot * TILE : (slot + 1) * TILE, LANES:] = shift
 
 
 def gather_kernel(
@@ -78,7 +84,6 @@
     rows_out,
     cols_out,
     weights_out,
-    bias_out,
     embed,
     weight,
     conv,
@@ -169,8 +174,7 @@
     def prepare():
         for load in loads[2:]:
             load.wait()
-        prepare_weights(conv, weights_out)
-        bias_out[0:LAYERS] = SCALE * jnp.concatenate([conv_bias[...], conv_bias[...]], axis=1)
+        prepare_weights(conv, conv_bias, weights_out)
 
     def chips_by_distance():
         flip = jnp.logical_or(z < NEAR // 2, z >= Z - NEAR // 2)
@@ -411,19 +415,19 @@
             self.copy(pair).wait()
 
 
-def conv_kernel(bands, rows, cols, weights, bias, out, staged, sems, *scratch):
+def conv_kernel(bands, rows, cols, weights, out, staged, sems, *scratch):
     offset = lax.axis_index("off")
 
     @pl.when(offset > 0)
     def _():
-        conv_layers(bands, offset, False, rows, cols, weights, bias, Writer(out, staged, sems), *scratch)
+        conv_layers(bands, offset, False, rows, cols, weights, Writer(out, staged, sems), *scratch)
 
     @pl.when(offset == 0)
     def _():
-        conv_layers(bands, offset, True, rows, cols, weights, bias, Writer(out, staged, sems), *scratch)
-
-
-def conv_layers(bands, offset, diagonal, rows, cols, weights, bias, out, state_a, state_b, hidden_a, hidden_b):
+        conv_layers(bands, offset, True, rows, cols, weights, Writer(out, staged, sems), *scratch)
+
+
+def conv_layers(bands, offset, diagonal, rows, cols, weights, out, state_a, state_b, hidden_a, hidden_b):
     def flag(holds):
         return jnp.broadcast_to(holds.astype(F32), (1, LANES))
 
@@ -440,7 +444,7 @@
 
     source, target = (state_a, hidden_a), (state_b, hidden_b)
     for layer in range(LAYERS):
-        conv_layer(layer, diagonal, source, target, weights.at[layer], bias[layer : layer + 1], out, inside, corner, start)
+        conv_layer(layer, diagonal, source, target, weights.at[layer], out, inside, corner, start)
         d = 2 ** (layer + 1)
         if layer == LAYERS - 1:
             out.end()
@@ -467,7 +471,7 @@
     return first, last
 
 
-def conv_layer(layer, diagonal, source, target, weights, bias, out, inside, corner, start):
+def conv_layer(layer, diagonal, source, target, weights, out, inside, corner, start):
     state, hidden = source
     next_state, next_hidden = target
     d = 2**layer
@@ -503,10 +507,14 @@
             tiles = inputs(quad)
             first, last = spans[quad]
             pieces = []
-            for step in (2 * part, min(2 * part + 1, 8)):
+            for step in (2 * part, 2 * part + 1):
                 row_tap, tile = divmod(step, 3)
-                pieces.append(hidden[pl.ds(at(tiles[tile], first + (row_tap - 1) * d), last - first), :])
-            lhs = jnp.concatenate(pieces, axis=1).astype(BF16)
+                if row_tap == 3:
+                    pieces.append(jnp.ones((last - first, LANES), BF16))
+                    continue
+                rows_in = pl.ds(at(tiles[tile], first + (row_tap - 1) * d), last - first)
+                pieces.append(hidden[rows_in, :].astype(BF16))
+            lhs = jnp.concatenate(pieces, axis=1)
             pltpu.matmul_acc_lhs(accs[places[turn, place]], lhs, part % 2 if place < 2 else None)
 
         def issue(turn):
@@ -522,8 +530,8 @@
             summed = pltpu.matmul_pop(accs[places[turn, place]])
             before, here, after = [state[tile, first:last] for tile in inputs(quad)]
             return [
-                summed[:, :LANES] + (halves(swap(before), here) + bias),
-                summed[:, LANES:] + (halves(here, swap(after)) + bias),
+                summed[:, :LANES] + halves(swap(before), here),
+                summed[:, LANES:] + halves(here, swap(after)),
             ]
 
         def finish(turn, place):
@@ -586,10 +594,9 @@
             pltpu.VMEM((SIDE, LANES), F32),
             pltpu.VMEM((MOST + 1, LANES), F32),
             pltpu.VMEM((LAYERS, PARTS, 256, 256), BF16),
-            pltpu.VMEM((8, LANES), F32),
         ],
         in_specs=[pl.BlockSpec(memory_space=pltpu.HBM)] * len(inputs),
-        out_specs=vmem(4),
+        out_specs=vmem(3),
         scratch_shapes=[
             *[
                 (pltpu.SMEM if value is block_slot else pltpu.VMEM)(value.shape, value.dtype)
@@ -608,7 +615,7 @@
         functools.partial(conv_kernel, bands),
         name="conv_tiles",
         out_shape=jax.ShapeDtypeStruct((1, 1, TILE, TILE * TILE), BF16),
-        in_specs=vmem(4),
+        in_specs=vmem(3),
         out_specs=pl.BlockSpec(memory_space=pl.ANY),
         scratch_shapes=[
             pltpu.VMEM((TILE, TILE * TILE), BF16),

time: 22 us -> 22 us (level)
  no operation moved by 1% of the time
where the time goes in v3:
time: 22 us; the launch traced here: 21.9 us
  Pallas kernels  21.7 us (99%)
    pallas_call x1, Pallas kernels, on_device(): pl.pallas_call(gather_kernel, name='gather_bins', out_shape=[pltpu.VMEM((...  14 us
    pallas_call x1, Pallas kernels, on_device(): pl.pallas_call(functools.partial(conv_kernel, bands), name='conv_tiles',...  7.72 us

profile of v3, /device:TPU:233, one launch (start us, length us, event | category | flops | bytes accessed | tf_op | source)
XLA Modules:
  0.0 21.9 jit_solution(14584543021813659678)
XLA Ops:
  0.0 14.0 %gather_bins.1 = (f32[96,128]{1,0:T(8,128)S(1)}, f32[48,128]{1,0:T(8,128)S(1)}, bf16[4,5,256,256]{3,2,1,0:T(8,128)(2,1)S(1)}) custom-call(bf16[64,128]{1,0:T(8,128)(2,1)} %embed_in.1, bf16[64,128]{1,0:T(8,128)(2,1)} %bitcast.4, bf16[4,64,576]{2,1,0:T(8,128)(2,1)} %bitcast.3, s32[32]{0:T(128)} %slots_in.1, f32[1,64]{1,0:T(1,128)} %bitcast.5, f32[4,64]{1,0:T(4,128)} %conv_bias_in.1), custom_call_target="tpu_custom_call" | custom-call | tf_op jit(solution)/shard_map/gather_bins/pallas_call | solution.py:590
  14.0 7.7 %conv_tiles.1 = bf16[1,1,64,4096]{3,2,1,0:T(8,128)(2,1)} custom-call(f32[96,128]{1,0:T(8,128)S(1)} %get-tuple-element.8.rows, f32[48,128]{1,0:T(8,128)S(1)} %get-tuple-element.9.cols, bf16[4,5,256,256]{3,2,1,0:T(8,128)(2,1)S(1)} %get-tuple-element.10.weights), custom_call_target="tpu_custom_call" | custom-call | tf_op jit(solution)/shard_map/conv_tiles/pallas_call | solution.py:614

commit v4 on v3

--- a/solution.py
+++ b/solution.py
@@ -245,10 +245,6 @@
 
     for chip in range(blocks // CORE):
         to_twin(2 * chip + 1 - core).wait_recv()
-    for chip in range(blocks // CORE):
-        to_twin(2 * chip + core).wait_send()
-    others(near_chips, lambda peer: to_peer(me, peer).wait_send())
-    others(far_chips, lambda peer: to_peer(me, peer).wait_send())
 
     def spread(base, out):
         def block(shift):
@@ -267,6 +263,10 @@
     left = cols[pl.ds(1, MOST, stride=2), :]
     right = cols[pl.ds(2, MOST, stride=2), :]
     cols_out[0:MOST] = halves(left, right) + SCALE * jnp.concatenate([bias[...], bias[...]], axis=1)
+    for chip in range(blocks // CORE):
+        to_twin(2 * chip + core).wait_send()
+    others(near_chips, lambda peer: to_peer(me, peer).wait_send())
+    others(far_chips, lambda peer: to_peer(me, peer).wait_send())
 
 
 def hide(value):

time: 22 us -> 22 us (level)
  no operation moved by 1% of the time
where the time goes in v4:
time: 22 us; the launch traced here: 21.9 us
  Pallas kernels  21.7 us (99%)
    pallas_call x1, Pallas kernels, on_device(): pl.pallas_call(gather_kernel, name='gather_bins', out_shape=[pltpu.VMEM((...  14 us
    pallas_call x1, Pallas kernels, on_device(): pl.pallas_call(functools.partial(conv_kernel, bands), name='conv_tiles',...  7.72 us

profile of v4, /device:TPU:233, one launch (start us, length us, event | category | flops | bytes accessed | tf_op | source)
XLA Modules:
  0.0 21.9 jit_solution(17947303819350171803)
XLA Ops:
  0.0 14.0 %gather_bins.1 = (f32[96,128]{1,0:T(8,128)S(1)}, f32[48,128]{1,0:T(8,128)S(1)}, bf16[4,5,256,256]{3,2,1,0:T(8,128)(2,1)S(1)}) custom-call(bf16[64,128]{1,0:T(8,128)(2,1)} %embed_in.1, bf16[64,128]{1,0:T(8,128)(2,1)} %bitcast.4, bf16[4,64,576]{2,1,0:T(8,128)(2,1)} %bitcast.3, s32[32]{0:T(128)} %slots_in.1, f32[1,64]{1,0:T(1,128)} %bitcast.5, f32[4,64]{1,0:T(4,128)} %conv_bias_in.1), custom_call_target="tpu_custom_call" | custom-call | tf_op jit(solution)/shard_map/gather_bins/pallas_call | solution.py:590
  14.0 7.7 %conv_tiles.1 = bf16[1,1,64,4096]{3,2,1,0:T(8,128)(2,1)} custom-call(f32[96,128]{1,0:T(8,128)S(1)} %get-tuple-element.8.rows, f32[48,128]{1,0:T(8,128)S(1)} %get-tuple-element.9.cols, bf16[4,5,256,256]{3,2,1,0:T(8,128)(2,1)S(1)} %get-tuple-element.10.weights), custom_call_target="tpu_custom_call" | custom-call | tf_op jit(solution)/shard_map/conv_tiles/pallas_call | solution.py:614
